TPU v7x, 32 devices: a whole 2x2x4 slice. The times are simulated.
32 devices in a mesh: row: 8 (over z, core), loop: 4 (over y, x).
Axes of the slice: x: 2, y: 2, z: 4, core: 2. Of those that a mesh axis runs over, the one named last changes fastest.
Arguments:
- student_image: bfloat16 [5120, 1024], P(('row', 'loop')), may hold values from -12 to 12
- student_text: bfloat16 [5120, 1024], P(('row', 'loop')), may hold values from -12 to 12
- teacher_image: bfloat16 [5120, 1024], P('row', 'loop'), may hold values from -12 to 12
- teacher_text: bfloat16 [5120, 1024], P('row', 'loop'), may hold values from -12 to 12
- student_scale: float32 [1], replicated, may hold values from 30 to 100
- teacher_scale: float32 [1], replicated, may hold values from 30 to 100
Outputs:
- loss: float32 [1], replicated
- grad_image: bfloat16 [5120, 1024], P(('row', 'loop'))
- grad_text: bfloat16 [5120, 1024], P(('row', 'loop'))
All inputs are finite; a program needn't handle non-finite values.
Results may differ from a plain program's by a relative error of at most 0.014.
The roundings to bfloat16 on the way count: a program that leaves them out, or rounds other values in their place, can miss the bound.
Values may be sent and summed in bfloat16 or wider, within the bound.
A program may use at most 128 MiB of HBM per device.

v0:
```python
import jax
import jax.numpy as jnp
from jax import lax
from jax.sharding import PartitionSpec as P

EPS = 1e-06


def unit_rows(codes):
    values = codes.astype(jnp.float32)
    norms = jnp.sqrt(jnp.sum(values * values, axis=1, keepdims=True) + EPS)
    return (values / norms, norms)


def back_norm(grad_unit, units, norms):
    inner = jnp.sum(grad_unit * units, axis=1, keepdims=True)
    return ((grad_unit - units * inner) / norms).astype(jnp.bfloat16)


def on_device(
    student_image, student_text, teacher_image, teacher_text, student_scale, teacher_scale
):
    simg_unit, simg_norm = unit_rows(student_image)
    stxt_unit, stxt_norm = unit_rows(student_text)
    simg_own = simg_unit.astype(jnp.bfloat16)
    stxt_own = stxt_unit.astype(jnp.bfloat16)
    timg_full = lax.all_gather(teacher_image, "loop", axis=1, tiled=True)
    timg = unit_rows(timg_full)[0].astype(jnp.bfloat16)
    ttxt_full = lax.all_to_all(teacher_text, "loop", split_axis=0, concat_axis=1, tiled=True)
    ttxt_own = unit_rows(ttxt_full)[0].astype(jnp.bfloat16)
    simg = lax.all_gather(simg_own, "loop", axis=0, tiled=True)
    stxt, ttxt = (
        lax.all_gather(stxt_own, "row", axis=0, tiled=True),
        lax.all_gather(ttxt_own, "row", axis=0, tiled=True),
    )
    sscale = student_scale[0]
    tscale = teacher_scale[0]
    slog = sscale * jnp.einsum("re,ce->rc", simg, stxt, preferred_element_type=jnp.float32)
    tlog = tscale * jnp.einsum("re,ce->rc", timg, ttxt, preferred_element_type=jnp.float32)
    smax, tmax = lax.pmax((jnp.max(slog, axis=1), jnp.max(tlog, axis=1)), "loop")
    sexp = jnp.exp(slog - smax[:, None])
    texp = jnp.exp(tlog - tmax[:, None])
    ssum, tsum, cross = lax.psum(
        (jnp.sum(sexp, axis=1), jnp.sum(texp, axis=1), jnp.sum(texp * (tlog - slog), axis=1)),
        "loop",
    )
    lses = smax + jnp.log(ssum)
    lset = tmax + jnp.log(tsum)
    diverge = cross / tsum - lset + lses
    group_total = lax.psum(jnp.sum(diverge), "row")
    batch_total = simg.shape[0] * lax.axis_size("row")
    loss = (group_total / batch_total).reshape(1)
    probs = jnp.exp(slog - lses[:, None])
    probt = jnp.exp(tlog - lset[:, None])
    grad_logits = (sscale * (probs - probt)).astype(jnp.bfloat16)
    dimg = lax.psum_scatter(
        jnp.dot(grad_logits, stxt, preferred_element_type=jnp.float32).astype(jnp.bfloat16),
        "loop",
        scatter_dimension=0,
        tiled=True,
    ).astype(jnp.float32)
    dtxt = lax.psum_scatter(
        jnp.einsum("rc,re->ce", grad_logits, simg, preferred_element_type=jnp.float32).astype(
            jnp.bfloat16
        ),
        "row",
        scatter_dimension=0,
        tiled=True,
    ).astype(jnp.float32)
    return (loss, back_norm(dimg, simg_unit, simg_norm), back_norm(dtxt, stxt_unit, stxt_norm))


def solution(mesh):
    return jax.shard_map(
        on_device,
        mesh=mesh,
        in_specs=(
            P(("row", "loop"), None),
            P(("row", "loop"), None),
            P("row", "loop"),
            P("row", "loop"),
            P(),
            P(),
        ),
        out_specs=(P(), P(("row", "loop"), None), P(("row", "loop"), None)),
        check_vma=False,
    )
```

profile of v0, /device:TPU:0, one launch (start us, length us, event | category | flops | bytes accessed | tf_op | source)
XLA Modules:
  0.0 265.1 jit_solution(4238910627074843657)
XLA Ops:
  7.2 0.7 all-gather.5.cloned.1.call-update
  8.0 1.1 fusion.5
  9.1 1.8 fusion.14
  10.9 0.0 all-gather.11.cloned.1.call-start
  11.0 1.1 fusion.6
  12.1 1.8 fusion.15
  14.0 14.7 %all_to_all.13 = bf16[4,160,256]{2,1,0:T(8,128)(2,1)S(1)} all-to-all(bf16[4,160,256]{2,1,0:T(8,128)(2,1)S(1)} %bitcast.19), channel_id=1, replica_groups=mesh['row'=8,'loop'=4] {'loop'}, dimensions={0} | all-to-all | bytes 655360 | tf_op jit(solution)/shard_map/all_to_all | solution.py:29
  28.8 0.1 copy.11
  28.8 0.1 fusion.13
  29.0 0.9 divide_convert_fusion
  31.2 12.3 %all-gather.5.cloned.1.call-done = bf16[640,1024]{1,0:T(8,128)(2,1)} async-done(((bf16[640,256]{1,0:T(8,128)(2,1)}), bf16[640,1024]{1,0:T(8,128)(2,1)}) %all-gather.5.cloned.1.call-update) | async-done | bytes 1310736 | tf_op jit(solution)/shard_map/all_gather | solution.py:27
  43.5 1.6 fusion.1
  45.2 29.5 %all-gather.9.cloned.1.call-done = bf16[640,1024]{1,0:T(8,128)(2,1)} async-done(((bf16[160,1024]{1,0:T(8,128)(2,1)}), bf16[640,1024]{1,0:T(8,128)(2,1)}) %all-gather.9.cloned.1.call-update) | async-done | bytes 1310736 | tf_op jit(solution)/shard_map/all_gather | solution.py:31
  74.6 35.4 %all-gather.11.cloned.1.call-done = bf16[1280,1024]{1,0:T(8,128)(2,1)} async-done(((bf16[160,1024]{1,0:T(8,128)(2,1)}), bf16[1280,1024]{1,0:T(8,128)(2,1)}) %all-gather.11.cloned.1.call-update) | async-done | bytes 2621456 | tf_op jit(solution)/shard_map/all_gather | solution.py:33
  110.0 4.2 %fusion.16 = (f32[640]{0:T(1024)S(1)}, f32[640,1280]{1,0:T(8,128)S(1)}) fusion(bf16[640,1024]{1,0:T(8,128)(2,1)} %all-gather.9.cloned.1.call-done, bf16[1280,1024]{1,0:T(8,128)(2,1)} %all-gather.11.cloned.1.call-done, f32[]{:T(128)} %bitcast.15), kind=kOutput, calls=%fused_computation.43 | convolution fusion | flops 1679359360 | bytes 7211524 | tf_op jit(solution)/shard_map/re,ce->rc/dot_general | solution.py:38
  114.2 30.8 %all-gather.7.cloned.1.call-done = bf16[1280,1024]{1,0:T(8,128)(2,1)} async-done(((bf16[160,1024]{1,0:T(8,128)(2,1)}), bf16[1280,1024]{1,0:T(8,128)(2,1)}) %all-gather.7.cloned.1.call-update) | async-done | bytes 2621456 | tf_op jit(solution)/shard_map/all_gather | solution.py:34
  144.9 5.8 %fusion.17 = (f32[640]{0:T(1024)S(1)}, f32[640,1280]{1,0:T(8,128)}) fusion(bf16[1280,1024]{1,0:T(8,128)(2,1)} %all-gather.7.cloned.1.call-done, bf16[640,1024]{1,0:T(8,128)(2,1)} %all-gather.5.cloned.1.call-done, f32[640]{0:T(1024)S(1)} %add_sqrt_fusion, f32[]{:T(128)} %bitcast.17), kind=kOutput, calls=%fused_computation.44 | convolution fusion | flops 1681325440 | bytes 7214084 | tf_op jit(solution)/shard_map/re,ce->rc/dot_general | solution.py:39
  150.7 10.0 %all-reduce.1 = (f32[640]{0:T(1024)S(1)}, f32[640]{0:T(1024)S(1)}) all-reduce(f32[640]{0:T(1024)S(1)} %get-tuple-element.14, f32[640]{0:T(1024)S(1)} %get-tuple-element.16), channel_id=1, replica_groups=mesh['row'=8,'loop'=4] {'loop'}, use_global_device_ids=true, to_apply=%region_11.0 | all-reduce | flops 1280 | bytes 10240 | tf_op jit(solution)/shard_map/pmax | solution.py:40
  160.7 3.3 %multiply_reduce_fusion = (f32[640]{0:T(1024)S(1)}, f32[640]{0:T(1024)S(1)}, f32[640]{0:T(1024)S(1)}) fusion(f32[640,1280]{1,0:T(8,128)} %get-tuple-element.17, f32[640,1280]{1,0:T(8,128)S(1)} %get-tuple-element.15, f32[640]{0:T(1024)S(1)} %get-tuple-element.10, f32[640]{0:T(1024)S(1)} %get-tuple-element.9), kind=kLoop, calls=%fused_computation.5 | loop fusion | flops 5732480 | bytes 6566400 | tf_op jit(solution)/shard_map/reduce_sum | solution.py:44
  164.0 14.0 %all-reduce = (f32[640]{0:T(1024)S(1)}, f32[640]{0:T(1024)S(1)}, f32[640]{0:T(1024)S(1)}) all-reduce(f32[640]{0:T(1024)S(1)} %get-tuple-element.5, f32[640]{0:T(1024)S(1)} %get-tuple-element.4, f32[640]{0:T(1024)S(1)} %get-tuple-element.3), channel_id=1, replica_groups=mesh['row'=8,'loop'=4] {'loop'}, use_global_device_ids=true, to_apply=%region_13.0 | all-reduce | flops 1920 | bytes 15360 | tf_op jit(solution)/shard_map/psum | solution.py:43
  178.1 0.6 add_reduce_fusion
  178.7 3.0 %multiply_convert_fusion = bf16[640,1280]{1,0:T(8,128)(2,1)S(1)} fusion(f32[640,1280]{1,0:T(8,128)} %get-tuple-element.17, f32[640,1280]{1,0:T(8,128)S(1)} %get-tuple-element.15, f32[640]{0:T(1024)S(1)} %get-tuple-element.12, f32[640]{0:T(1024)S(1)} %get-tuple-element.13, f32[]{:T(128)} %bitcast.16), kind=kLoop, calls=%fused_computation.3 | loop fusion | flops 4096000 | bytes 8197124 | tf_op jit(solution)/shard_map/convert_element_type | solution.py:55
  181.7 1.2 copy-done.2
  182.9 3.0 %convolution_convert_fusion.1 = bf16[640,1024]{1,0:T(8,128)(2,1)} fusion(bf16[640,1280]{1,0:T(8,128)(2,1)S(1)} %multiply_convert_fusion, bf16[1280,1024]{1,0:T(8,128)(2,1)S(1)} %copy-done.4), kind=kOutput, calls=%fused_computation.12 | convolution fusion | flops 1678376960 | bytes 5570560 | tf_op jit(solution)/shard_map/dot_general | solution.py:57
  186.0 5.2 %convolution_convert_fusion = bf16[1280,1024]{1,0:T(8,128)(2,1)} fusion(bf16[640,1280]{1,0:T(8,128)(2,1)} %copy-done.2, bf16[640,1024]{1,0:T(8,128)(2,1)S(1)} %copy-done.5), kind=kOutput, calls=%fused_computation | convolution fusion | flops 1679032320 | bytes 5570560 | tf_op jit(solution)/shard_map/rc,re->ce/dot_general | solution.py:63
  191.2 14.2 %psum.31 = f32[]{:T(128)} all-reduce(f32[]{:T(128)} %get-tuple-element.11), channel_id=1, replica_groups=mesh['row'=8,'loop'=4] {'row'}, use_global_device_ids=true, to_apply=%region_15.0 | all-reduce | flops 1 | bytes 8 | tf_op jit(solution)/shard_map/psum | solution.py:50
  206.1 7.7 %reduce-scatter.3.cloned.1.call-done = bf16[160,1024]{1,0:T(8,128)(2,1)} async-done(((bf16[640,1024]{1,0:T(8,128)(2,1)}), bf16[160,1024]{1,0:T(8,128)(2,1)}) %reduce-scatter.3.cloned.1.call-update) | async-done | bytes 327696 | tf_op jit(solution)/shard_map/reduce_scatter | solution.py:56
  213.8 1.2 fusion.7
  215.0 2.0 fusion.9
  217.0 37.0 %reduce-scatter.5.cloned.1.call-done = bf16[160,1024]{1,0:T(8,128)(2,1)} async-done(((bf16[1280,1024]{1,0:T(8,128)(2,1)}), bf16[160,1024]{1,0:T(8,128)(2,1)}) %reduce-scatter.5.cloned.1.call-update) | async-done | bytes 327696 | tf_op jit(solution)/shard_map/reduce_scatter | solution.py:62
  253.9 1.2 fusion.10
  255.2 2.0 fusion.12
  (26 shorter events, 0.4 us)
Async XLA Ops:
  7.2 6.9 %copy-start.3 = (bf16[640,256]{1,0:T(8,128)(2,1)S(1)}, bf16[640,256]{1,0:T(8,128)(2,1)}, u32[]{:S(2)}) copy-start(bf16[640,256]{1,0:T(8,128)(2,1)} %param.9) | copy-start | bytes 983044
  7.2 36.3 %all-gather.5.cloned.1.call-start = ((), (), s32[]{:S(2)}) async-start(), calls=%async_computation.3 | async-start | bytes 1638400 | tf_op jit(solution)/shard_map/all_gather | solution.py:27
  7.9 66.7 %all-gather.9.cloned.1.call-start = ((), (), s32[]{:S(2)}) async-start(), calls=%async_computation.5 | async-start | bytes 1638400 | tf_op jit(solution)/shard_map/all_gather | solution.py:31
  10.9 99.1 %all-gather.11.cloned.1.call-start = ((), (), s32[]{:S(2)}) async-start(), calls=%async_computation.6 | async-start | bytes 2949120 | tf_op jit(solution)/shard_map/all_gather | solution.py:33
  14.0 131.0 %all-gather.7.cloned.1.call-start = ((), (), s32[]{:S(2)}) async-start(), calls=%async_computation.4 | async-start | bytes 2949120 | tf_op jit(solution)/shard_map/all_gather | solution.py:34
  29.9 183.9 %reduce-scatter.3.cloned.1.call-start = ((), (), s32[]{:S(2)}) async-start(), calls=%async_computation.7 | async-start | bytes 1638400 | tf_op jit(solution)/shard_map/reduce_scatter | solution.py:56
  178.7 4.2 %copy-start.4 = (bf16[1280,1024]{1,0:T(8,128)(2,1)S(1)}, bf16[1280,1024]{1,0:T(8,128)(2,1)}, u32[]{:S(2)}) copy-start(bf16[1280,1024]{1,0:T(8,128)(2,1)} %all-gather.11.cloned.1.call-done) | copy-start | bytes 7864324
  181.7 1.2 copy-start.2
  182.9 3.1 %copy-start.5 = (bf16[640,1024]{1,0:T(8,128)(2,1)S(1)}, bf16[640,1024]{1,0:T(8,128)(2,1)}, u32[]{:S(2)}) copy-start(bf16[640,1024]{1,0:T(8,128)(2,1)} %all-gather.9.cloned.1.call-done) | copy-start | bytes 3932164
  185.9 68.0 %reduce-scatter.5.cloned.1.call-start = ((), (), s32[]{:S(2)}) async-start(), calls=%async_computation.8 | async-start | bytes 2949120 | tf_op jit(solution)/shard_map/reduce_scatter | solution.py:62
  191.2 22.6 %copy-start = (bf16[160,1024]{1,0:T(8,128)(2,1)S(1)}, bf16[160,1024]{1,0:T(8,128)(2,1)}, u32[]{:S(2)}) copy-start(bf16[160,1024]{1,0:T(8,128)(2,1)} %param.6) | copy-start | bytes 983044
  191.2 62.8 %copy-start.1 = (bf16[160,1024]{1,0:T(8,128)(2,1)S(1)}, bf16[160,1024]{1,0:T(8,128)(2,1)}, u32[]{:S(2)}) copy-start(bf16[160,1024]{1,0:T(8,128)(2,1)} %param.7) | copy-start | bytes 983044
Sparse Core Ops, SparseCore 0:
  9.8 33.6 all-gather.4
  45.9 28.6 all-gather.8
  76.3 33.6 all-gather.10
  112.1 32.8 all-gather.6
  186.0 27.6 reduce-scatter.2
  215.9 37.9 reduce-scatter.4
where the time goes:
time: 266 us; the launch traced here: 265 us
  waiting for transfers between devices  153 us (58%)
  blocking collectives  52.9 us (20%)
  other arithmetic  22 us (8%)
  matrix products  18.1 us (7%)
  between operations  17.3 us (7%)
    reduce_scatter x1, waiting for transfers between devices, on_device(): lax.psum_scatter(jnp.einsum('rc,re->ce', grad_logits, simg, preferred_ele...  37 us
    all_gather x1, waiting for transfers between devices, on_device(): lax.all_gather(stxt_own, 'row', axis=0, tiled=True)  35.4 us
    all_gather x1, waiting for transfers between devices, on_device(): lax.all_gather(ttxt_own, 'row', axis=0, tiled=True)  30.8 us
    all_gather x1, waiting for transfers between devices, on_device(): simg = lax.all_gather(simg_own, 'loop', axis=0, tiled=True)  29.5 us
    all_to_all x1, blocking collectives, on_device(): lax.all_to_all(teacher_text, 'loop', split_axis=0, concat_axis=1, tiled=T...  14.7 us
    psum x1, blocking collectives, on_device(): group_total = lax.psum(jnp.sum(diverge), 'row')  14.2 us
    psum x1, blocking collectives, on_device(): lax.psum((jnp.sum(sexp, axis=1), jnp.sum(texp, axis=1), jnp.sum(texp * (t...  14 us
    all_gather x1, waiting for transfers between devices, on_device(): timg_full = lax.all_gather(teacher_image, 'loop', axis=1, tiled=True)  12.3 us
  transfers between devices with their start and end apart: 6, of which 6 were waited for; matrix products, arithmetic and copies ran while one was open for 8% of the time, Pallas kernels for 0%

commit v1 on v0

--- a/solution.py
+++ b/solution.py
@@ -4,6 +4,23 @@
 from jax.sharding import PartitionSpec as P
 
 EPS = 1e-06
+
+
+def counts_meet(block_in):
+    steps_seen = []
+    w = 0
+    p_count = lax.axis_size("loop")
+    while w < p_count:
+        steps_seen.append((w, (w + 1) % p_count))
+        w += 1
+
+    def get_keys(row_out):
+        if len(row_out) == p_count:
+            return row_out
+        return get_keys([lax.ppermute(row_out[0], axis_name="loop", perm=steps_seen), *row_out])
+
+    parts_out = jnp.concatenate(get_keys([block_in]), 0)
+    return jnp.roll(parts_out, (lax.axis_index("loop") + 1) * block_in.shape[0], 0)
 
 
 def unit_rows(codes):
@@ -28,7 +45,7 @@
     timg = unit_rows(timg_full)[0].astype(jnp.bfloat16)
     ttxt_full = lax.all_to_all(teacher_text, "loop", split_axis=0, concat_axis=1, tiled=True)
     ttxt_own = unit_rows(ttxt_full)[0].astype(jnp.bfloat16)
-    simg = lax.all_gather(simg_own, "loop", axis=0, tiled=True)
+    simg = counts_meet(simg_own)
     stxt, ttxt = (
         lax.all_gather(stxt_own, "row", axis=0, tiled=True),
         lax.all_gather(ttxt_own, "row", axis=0, tiled=True),

time: 266 us -> 239 us (0.90)
  waiting for transfers between devices: 153 us -> 125 us
  local copies, waits for them, and re-layouts: 1.26 us -> 5.85 us
  blocking collectives: 52.9 us -> 50.2 us
    ppermute x0 -> x3, waiting for transfers between devices: none -> 32.2 us  [get_keys(): lax.ppermute(row_out[0], axis_name='loop', perm=steps_seen)]
    all_gather x1 -> x0, waiting for transfers between devices: 29.5 us -> none  [on_device(): simg = lax.all_gather(simg_own, 'loop', axis=0, tiled=True)]
    all_gather x1, waiting for transfers between devices: 35.4 us -> 16.9 us  [on_device(): lax.all_gather(stxt_own, 'row', axis=0, tiled=True)]
    all_gather x1, waiting for transfers between devices: 12.3 us -> 0.01 us  [on_device(): timg_full = lax.all_gather(teacher_image, 'loop', axis=1, tiled=True)]
    unnamed x12 -> x16, local copies, waits for them, and re-layouts: 1.2 us -> 5.78 us
    all_to_all x1, blocking collectives: 14.7 us -> 11.9 us  [on_device(): lax.all_to_all(teacher_text, 'loop', split_axis=0, concat_axis=1, tiled=T...]
  transfers between devices with their start and end apart: 6 -> 8, of which waited for: 6 -> 7; matrix products, arithmetic and copies ran while one was open for 8% -> 11% of each run, Pallas kernels for 0% -> 0%
where the time goes in v1:
time: 239 us; the launch traced here: 238 us
  waiting for transfers between devices  125 us (52%)
  blocking collectives  50.2 us (21%)
  other arithmetic  21 us (9%)
  matrix products  18.5 us (8%)
  between operations  16.9 us (7%)
  local copies, waits for them, and re-layouts  5.85 us (2%)
    reduce_scatter x1, waiting for transfers between devices, on_device(): lax.psum_scatter(jnp.einsum('rc,re->ce', grad_logits, simg, preferred_ele...  36.8 us
    ppermute x3, waiting for transfers between devices, get_keys(): lax.ppermute(row_out[0], axis_name='loop', perm=steps_seen)  32.2 us
    all_gather x1, waiting for transfers between devices, on_device(): lax.all_gather(ttxt_own, 'row', axis=0, tiled=True)  30.9 us
    all_gather x1, waiting for transfers between devices, on_device(): lax.all_gather(stxt_own, 'row', axis=0, tiled=True)  16.9 us
    psum x1, blocking collectives, on_device(): group_total = lax.psum(jnp.sum(diverge), 'row')  14.2 us
    psum x1, blocking collectives, on_device(): lax.psum((jnp.sum(sexp, axis=1), jnp.sum(texp, axis=1), jnp.sum(texp * (t...  14 us
    all_to_all x1, blocking collectives, on_device(): lax.all_to_all(teacher_text, 'loop', split_axis=0, concat_axis=1, tiled=T...  11.9 us
    pmax x1, blocking collectives, on_device(): lax.pmax((jnp.max(slog, axis=1), jnp.max(tlog, axis=1)), 'loop')  9.97 us
  transfers between devices with their start and end apart: 8, of which 7 were waited for; matrix products, arithmetic and copies ran while one was open for 11% of the time, Pallas kernels for 0%

profile of v1, /device:TPU:0, one launch (start us, length us, event | category | flops | bytes accessed | tf_op | source)
XLA Modules:
  0.0 238.3 jit_solution(4907904773538077246)
XLA Ops:
  7.9 1.1 fusion.8
  9.1 1.8 fusion.19
  11.0 11.9 %all_to_all.13 = bf16[4,160,256]{2,1,0:T(8,128)(2,1)S(1)} all-to-all(bf16[4,160,256]{2,1,0:T(8,128)(2,1)} %bitcast.17), channel_id=1, replica_groups=mesh['row'=8,'loop'=4] {'loop'}, dimensions={0} | all-to-all | bytes 655360 | tf_op jit(solution)/shard_map/all_to_all | solution.py:46
  23.2 0.9 divide_convert_fusion
  24.4 0.8 collective-permute-start
  25.2 8.8 %collective-permute-done = bf16[160,1024]{1,0:T(8,128)(2,1)S(1)} collective-permute-done((bf16[160,1024]{1,0:T(8,128)(2,1)S(1)}, bf16[160,1024]{1,0:T(8,128)(2,1)S(1)}, u32[]{:S(2)}, u32[]{:S(2)}) %collective-permute-start) | collective-permute-done | bytes 327712 | tf_op jit(solution)/shard_map/ppermute | solution.py:20
  34.1 15.0 %collective-permute-done.1 = bf16[160,1024]{1,0:T(8,128)(2,1)S(1)} collective-permute-done((bf16[160,1024]{1,0:T(8,128)(2,1)S(1)}, bf16[160,1024]{1,0:T(8,128)(2,1)S(1)}, u32[]{:S(2)}, u32[]{:S(2)}) %collective-permute-start.1) | collective-permute-done | bytes 327712 | tf_op jit(solution)/shard_map/ppermute | solution.py:20
  50.4 8.3 %collective-permute-done.2 = bf16[160,1024]{1,0:T(8,128)(2,1)S(1)} collective-permute-done((bf16[160,1024]{1,0:T(8,128)(2,1)S(1)}, bf16[160,1024]{1,0:T(8,128)(2,1)S(1)}, u32[]{:S(2)}, u32[]{:S(2)}) %collective-permute-start.2) | collective-permute-done | bytes 327712 | tf_op jit(solution)/shard_map/ppermute | solution.py:20
  58.7 0.8 constant_dynamic-update-slice_fusion.7
  59.5 0.8 constant_dynamic-update-slice_fusion.6
  60.3 0.8 constant_dynamic-update-slice_fusion.5
  61.0 0.8 constant_dynamic-update-slice_fusion.4
  64.1 0.9 constant_dynamic-update-slice_fusion
  65.0 1.6 fusion.1
  66.7 16.9 %all-gather.8.cloned.1.call-done = bf16[1280,1024]{1,0:T(8,128)(2,1)} async-done(((bf16[160,1024]{1,0:T(8,128)(2,1)}), bf16[1280,1024]{1,0:T(8,128)(2,1)}) %all-gather.8.cloned.1.call-update) | async-done | bytes 2621456 | tf_op jit(solution)/shard_map/all_gather | solution.py:50
  83.5 4.2 %fusion.20 = (f32[640]{0:T(1024)S(1)}, f32[640,1280]{1,0:T(8,128)S(1)}) fusion(bf16[1280,1024]{1,0:T(8,128)(2,1)} %all-gather.8.cloned.1.call-done, bf16[1280,1024]{1,0:T(8,128)(2,1)} %constant_dynamic-update-slice_fusion, s32[]{:T(128)S(6)} %select_n.14, f32[]{:T(128)} %bitcast.13), kind=kOutput, calls=%fused_computation.55 | convolution fusion | flops 1679359360 | bytes 7212036 | tf_op jit(solution)/shard_map/re,ce->rc/dot_general | solution.py:55
  87.7 30.9 %all-gather.6.cloned.1.call-done = bf16[1280,1024]{1,0:T(8,128)(2,1)} async-done(((bf16[160,1024]{1,0:T(8,128)(2,1)}), bf16[1280,1024]{1,0:T(8,128)(2,1)}) %all-gather.6.cloned.1.call-update) | async-done | bytes 2621456 | tf_op jit(solution)/shard_map/all_gather | solution.py:51
  118.6 5.8 %fusion.21 = (f32[640]{0:T(1024)S(1)}, f32[640,1280]{1,0:T(8,128)}) fusion(bf16[1280,1024]{1,0:T(8,128)(2,1)} %all-gather.6.cloned.1.call-done, bf16[640,1024]{1,0:T(8,128)(2,1)} %all-gather.4.cloned.1.call-done, f32[640]{0:T(1024)S(1)} %add_sqrt_fusion, f32[]{:T(128)} %bitcast.15), kind=kOutput, calls=%fused_computation.56 | convolution fusion | flops 1681325440 | bytes 7214084 | tf_op jit(solution)/shard_map/re,ce->rc/dot_general | solution.py:56
  124.4 10.0 %all-reduce.1 = (f32[640]{0:T(1024)S(1)}, f32[640]{0:T(1024)S(1)}) all-reduce(f32[640]{0:T(1024)S(1)} %get-tuple-element.14, f32[640]{0:T(1024)S(1)} %get-tuple-element.16), channel_id=1, replica_groups=mesh['row'=8,'loop'=4] {'loop'}, use_global_device_ids=true, to_apply=%region_11.12 | all-reduce | flops 1280 | bytes 10240 | tf_op jit(solution)/shard_map/pmax | solution.py:57
  134.4 3.3 %multiply_reduce_fusion = (f32[640]{0:T(1024)S(1)}, f32[640]{0:T(1024)S(1)}, f32[640]{0:T(1024)S(1)}) fusion(f32[640,1280]{1,0:T(8,128)} %get-tuple-element.17, f32[640,1280]{1,0:T(8,128)S(1)} %get-tuple-element.15, f32[640]{0:T(1024)S(1)} %get-tuple-element.10, f32[640]{0:T(1024)S(1)} %get-tuple-element.9), kind=kLoop, calls=%fused_computation.5 | loop fusion | flops 5732480 | bytes 6566400 | tf_op jit(solution)/shard_map/reduce_sum | solution.py:61
  137.7 14.0 %all-reduce = (f32[640]{0:T(1024)S(1)}, f32[640]{0:T(1024)S(1)}, f32[640]{0:T(1024)S(1)}) all-reduce(f32[640]{0:T(1024)S(1)} %get-tuple-element.5, f32[640]{0:T(1024)S(1)} %get-tuple-element.4, f32[640]{0:T(1024)S(1)} %get-tuple-element.3), channel_id=1, replica_groups=mesh['row'=8,'loop'=4] {'loop'}, use_global_device_ids=true, to_apply=%region_13.14 | all-reduce | flops 1920 | bytes 15360 | tf_op jit(solution)/shard_map/psum | solution.py:60
  152.3 3.0 %multiply_convert_fusion = bf16[640,1280]{1,0:T(8,128)(2,1)S(1)} fusion(f32[640,1280]{1,0:T(8,128)} %get-tuple-element.17, f32[640,1280]{1,0:T(8,128)S(1)} %get-tuple-element.15, f32[640]{0:T(1024)S(1)} %get-tuple-element.12, f32[640]{0:T(1024)S(1)} %get-tuple-element.13, f32[]{:T(128)} %bitcast.14), kind=kLoop, calls=%fused_computation.3 | loop fusion | flops 4096000 | bytes 8197124 | tf_op jit(solution)/shard_map/convert_element_type | solution.py:72
  155.4 1.2 copy-done.3
  156.6 3.0 %convolution_convert_fusion.1 = bf16[640,1024]{1,0:T(8,128)(2,1)} fusion(bf16[640,1280]{1,0:T(8,128)(2,1)S(1)} %multiply_convert_fusion, bf16[1280,1024]{1,0:T(8,128)(2,1)S(1)} %copy-done.4), kind=kOutput, calls=%fused_computation.12 | convolution fusion | flops 1678376960 | bytes 5570560 | tf_op jit(solution)/shard_map/dot_general | solution.py:74
  159.6 5.6 %convolution_convert_fusion = bf16[1280,1024]{1,0:T(8,128)(2,1)} fusion(bf16[640,1280]{1,0:T(8,128)(2,1)} %copy-done.3, bf16[1280,1024]{1,0:T(8,128)(2,1)} %constant_dynamic-update-slice_fusion, s32[]{:T(128)S(6)} %select_n.14), kind=kOutput, calls=%fused_computation | convolution fusion | flops 1679032320 | bytes 5570564 | tf_op jit(solution)/shard_map/rc,re->ce/dot_general | solution.py:80
  165.2 14.2 %psum.31 = f32[]{:T(128)} all-reduce(f32[]{:T(128)} %get-tuple-element.11), channel_id=1, replica_groups=mesh['row'=8,'loop'=4] {'row'}, use_global_device_ids=true, to_apply=%region_15.16 | all-reduce | flops 1 | bytes 8 | tf_op jit(solution)/shard_map/psum | solution.py:67
  180.1 7.3 %reduce-scatter.3.cloned.1.call-done = bf16[160,1024]{1,0:T(8,128)(2,1)} async-done(((bf16[640,1024]{1,0:T(8,128)(2,1)}), bf16[160,1024]{1,0:T(8,128)(2,1)}) %reduce-scatter.3.cloned.1.call-update) | async-done | bytes 327696 | tf_op jit(solution)/shard_map/reduce_scatter | solution.py:73
  187.4 1.2 fusion.9
  188.7 2.0 fusion.11
  190.6 36.8 %reduce-scatter.5.cloned.1.call-done = bf16[160,1024]{1,0:T(8,128)(2,1)} async-done(((bf16[1280,1024]{1,0:T(8,128)(2,1)}), bf16[160,1024]{1,0:T(8,128)(2,1)}) %reduce-scatter.5.cloned.1.call-update) | async-done | bytes 327696 | tf_op jit(solution)/shard_map/reduce_scatter | solution.py:79
  227.4 1.2 fusion.12
  228.7 2.0 fusion.14
  (35 shorter events, 4.4 us)
Async XLA Ops:
  7.2 57.8 %all-gather.4.cloned.1.call-start = ((), (), s32[]{:S(2)}) async-start(), calls=%async_computation.3 | async-start | bytes 1638400 | tf_op jit(solution)/shard_map/all_gather | solution.py:44
  7.9 75.6 %all-gather.8.cloned.1.call-start = ((), (), s32[]{:S(2)}) async-start(), calls=%async_computation.5 | async-start | bytes 2949120 | tf_op jit(solution)/shard_map/all_gather | solution.py:50
  10.9 13.2 %copy-start = (bf16[160,1024]{1,0:T(8,128)(2,1)S(1)}, bf16[160,1024]{1,0:T(8,128)(2,1)}, u32[]{:S(2)}) copy-start(bf16[160,1024]{1,0:T(8,128)(2,1)} %param.6) | copy-start | bytes 983044
  10.9 107.7 %all-gather.6.cloned.1.call-start = ((), (), s32[]{:S(2)}) async-start(), calls=%async_computation.4 | async-start | bytes 2949120 | tf_op jit(solution)/shard_map/all_gather | solution.py:51
  24.1 163.4 %reduce-scatter.3.cloned.1.call-start = ((), (), s32[]{:S(2)}) async-start(), calls=%async_computation.6 | async-start | bytes 1638400 | tf_op jit(solution)/shard_map/reduce_scatter | solution.py:73
  24.4 9.6 %collective-permute-start = (bf16[160,1024]{1,0:T(8,128)(2,1)S(1)}, bf16[160,1024]{1,0:T(8,128)(2,1)S(1)}, u32[]{:S(2)}, u32[]{:S(2)}) collective-permute-start(bf16[160,1024]{1,0:T(8,128)(2,1)S(1)} %fusion.18), channel_id=1, source_target_pairs={{0,1},{1,2},{2,3},{3,0},{4,5},{5,6},{6,7},{7,4},{8,9},{9,10},{10,1... | collective-permute-start | bytes 983048 | tf_op jit(solution)/shard_map/ppermute | solution.py:20
  34.1 15.0 %collective-permute-start.1 = (bf16[160,1024]{1,0:T(8,128)(2,1)S(1)}, bf16[160,1024]{1,0:T(8,128)(2,1)S(1)}, u32[]{:S(2)}, u32[]{:S(2)}) collective-permute-start(bf16[160,1024]{1,0:T(8,128)(2,1)S(1)} %collective-permute-done), channel_id=1, source_target_pairs={{0,1},{1,2},{2,3},{3,0},{4,5},{5,6},{6,7},{7,4},{8,9},{9,10},{10,1... | collective-permute-start | bytes 983048 | tf_op jit(solution)/shard_map/ppermute | solution.py:20
  49.1 9.6 %collective-permute-start.2 = (bf16[160,1024]{1,0:T(8,128)(2,1)S(1)}, bf16[160,1024]{1,0:T(8,128)(2,1)S(1)}, u32[]{:S(2)}, u32[]{:S(2)}) collective-permute-start(bf16[160,1024]{1,0:T(8,128)(2,1)S(1)} %collective-permute-done.1), channel_id=1, source_target_pairs={{0,1},{1,2},{2,3},{3,0},{4,5},{5,6},{6,7},{7,4},{8,9},{9,10},{10,1... | collective-permute-start | bytes 983048 | tf_op jit(solution)/shard_map/ppermute | solution.py:20
  152.3 4.2 %copy-start.4 = (bf16[1280,1024]{1,0:T(8,128)(2,1)S(1)}, bf16[1280,1024]{1,0:T(8,128)(2,1)}, u32[]{:S(2)}) copy-start(bf16[1280,1024]{1,0:T(8,128)(2,1)} %all-gather.8.cloned.1.call-done) | copy-start | bytes 7864324
  155.4 1.2 copy-start.3
  159.6 67.9 %reduce-scatter.5.cloned.1.call-start = ((), (), s32[]{:S(2)}) async-start(), calls=%async_computation.7 | async-start | bytes 2949120 | tf_op jit(solution)/shard_map/reduce_scatter | solution.py:79
  165.2 22.2 %copy-start.1 = (bf16[160,1024]{1,0:T(8,128)(2,1)S(1)}, bf16[160,1024]{1,0:T(8,128)(2,1)}, u32[]{:S(2)}) copy-start(bf16[160,1024]{1,0:T(8,128)(2,1)} %param.6) | copy-start | bytes 983044
  165.2 62.2 %copy-start.2 = (bf16[160,1024]{1,0:T(8,128)(2,1)S(1)}, bf16[160,1024]{1,0:T(8,128)(2,1)}, u32[]{:S(2)}) copy-start(bf16[160,1024]{1,0:T(8,128)(2,1)} %param.7) | copy-start | bytes 983044
Sparse Core Ops, SparseCore 0:
  9.8 37.4 all-gather.3
  49.5 33.9 all-gather.7
  85.7 32.8 all-gather.5
  159.7 27.6 reduce-scatter.2
  189.6 37.8 reduce-scatter.4
